TPU v7x, 512 devices: a whole 4x8x8 slice. The times are simulated.
512 devices in a mesh: batch: 4 (over x_hi, core), space: 128 (over x_lo, y, z).
Axes of the slice: x: 4 (x_hi: 2, x_lo: 2; x = x_hi * 2 + x_lo), y: 8, z: 8, core: 2. Of those that a mesh axis runs over, the one named last changes fastest.
Arguments:
- inputs: bfloat16 [4, 32, 128, 128, 128], P('batch', None, None, 'space'), may hold values from -6 to 6
- pre_act: bfloat16 [4, 32, 128, 128, 128], P('batch', None, None, 'space'), may hold values from -8 to 8
- cotangent: bfloat16 [4, 32, 128, 128, 128], P('batch', None, None, 'space'), may hold values from -6 to 6
- spectral_weight: bfloat16 [2, 32, 32, 16384], P(None, None, None, 'space'), may hold values from -6 to 6
- skip_weight: bfloat16 [32, 32], replicated, may hold values from -1 to 1
Outputs:
- grad_inputs: bfloat16 [4, 32, 128, 128, 128], P('batch', None, None, 'space')
- grad_spectral: float32 [2, 32, 32, 16384], P(None, None, 'batch', 'space')
- grad_skip: float32 [32, 32], replicated
All inputs are finite; a program needn't handle non-finite values.
Results may differ from a plain program's by a relative error of at most 0.0055.
Values sent between devices are 32-bit elements; how exact they have to be, the bound alone decides.
A program may use at most 64 MiB of HBM per device.

v0:
```python
import math
import jax
import jax.numpy as jnp
from jax import lax
from jax.sharding import PartitionSpec as P

NX = 128
NY = 128
NZ = 128
MX = 16
MY = 16
MZ = 16
HIGHEST = lax.Precision.HIGHEST


def phase_table(length, count, signed):
    points = jnp.arange(length, dtype=jnp.int32)
    orders = jnp.arange(count, dtype=jnp.int32)
    if signed:
        orders = jnp.where(orders < count // 2, orders, orders - count)
    residues = jnp.mod(points[:, None] * orders[None, :], length)
    radians = residues.astype(jnp.float32) * (2.0 * math.pi / length)
    return (jnp.cos(radians), jnp.sin(radians))


def forward_block(cosine, sine):
    return jnp.stack(
        [jnp.stack([cosine, -sine], axis=1), jnp.stack([sine, cosine], axis=1)], axis=0
    )


def inverse_block(cosine, sine):
    cos_rows = cosine.T
    sin_rows = sine.T
    return jnp.stack(
        [jnp.stack([cos_rows, sin_rows], axis=1), jnp.stack([-sin_rows, cos_rows], axis=1)], axis=0
    )


def gelu_slope(values):
    normal_cdf = 0.5 * (1.0 + jax.scipy.special.erf(values * (1.0 / math.sqrt(2.0))))
    density = jnp.exp(-0.5 * values * values) * (1.0 / math.sqrt(2.0 * math.pi))
    return normal_cdf + values * density


def local_spectrum(grid_in):
    cos_x, sin_x = phase_table(NX, 2 * MX, True)
    table_x = jnp.stack([cos_x, -sin_x], axis=1).astype(jnp.bfloat16)
    section_x = jnp.einsum(
        "scxyz,xpa->scpayz", grid_in, table_x, preferred_element_type=jnp.float32
    )
    cos_z, sin_z = phase_table(NZ, MZ, False)
    section_z = jnp.einsum(
        "scpayz,pzqk->scqyak", section_x, forward_block(cos_z, sin_z), precision=HIGHEST
    )
    return section_z.reshape(
        section_z.shape[0], section_z.shape[1], 2, section_z.shape[3], 2 * MX * MZ
    )


def along_y(spectra):
    cos_y, sin_y = phase_table(NY, 2 * MY, True)
    section_y = jnp.einsum(
        "scpym,pyqk->scqmk", spectra, forward_block(cos_y, sin_y), precision=HIGHEST
    )
    return section_y.reshape(section_y.shape[0], section_y.shape[1], 2, section_y.shape[3] * 2 * MY)


def both_along_y(spectra_pair):
    return (along_y(spectra_pair[0]), along_y(spectra_pair[1]))


def to_grid(spectra):
    shaped = spectra.reshape(spectra.shape[0], spectra.shape[1], 2, spectra.shape[3], 2 * MX, MZ)
    cos_z, sin_z = phase_table(NZ, MZ, False)
    grid_z = jnp.einsum(
        "scpyak,pkqz->scqayz", shaped, inverse_block(cos_z, sin_z), precision=HIGHEST
    )
    cos_x, sin_x = phase_table(NX, 2 * MX, True)
    table_x = jnp.stack([cos_x.T, -sin_x.T], axis=0)
    return jnp.einsum("scpayz,pax->scxyz", grid_z, table_x, precision=HIGHEST)


def cross_terms(spec_left, spec_right):
    real_part = jnp.einsum(
        "sim,som->iom", spec_left[:, :, 0], spec_right[:, :, 0], precision=HIGHEST
    )
    real_part = real_part + jnp.einsum(
        "sim,som->iom", spec_left[:, :, 1], spec_right[:, :, 1], precision=HIGHEST
    )
    imag_part = jnp.einsum(
        "sim,som->iom", spec_left[:, :, 0], spec_right[:, :, 1], precision=HIGHEST
    )
    imag_part = imag_part - jnp.einsum(
        "sim,som->iom", spec_left[:, :, 1], spec_right[:, :, 0], precision=HIGHEST
    )
    return jnp.stack([real_part, imag_part], axis=0)


def contract(weight_part, spec_part):
    return jnp.einsum("iom,som->sim", weight_part, spec_part, preferred_element_type=jnp.float32)


def skip_gradient(grid_in, cot_pre):
    partial_sum = jnp.einsum(
        "sixyz,soxyz->io", grid_in, cot_pre, preferred_element_type=jnp.float32
    )
    summed = lax.psum(partial_sum, ("batch", "space"))
    return summed / math.sqrt(grid_in.shape[0] * lax.axis_size("batch") * NX * NY * NZ)


def on_device(inputs, pre_act, cotangent, spectral_weight, skip_weight):
    samples = inputs.shape[0]
    channels = inputs.shape[1]
    slope_pre = gelu_slope(pre_act.astype(jnp.float32))
    cot_pre = (cotangent.astype(jnp.float32) * slope_pre).astype(jnp.bfloat16)
    spec_u, spec_e = both_along_y(
        (
            lax.all_to_all(
                local_spectrum(inputs), "space", split_axis=4, concat_axis=3, tiled=True
            ),
            lax.all_to_all(
                local_spectrum(cot_pre), "space", split_axis=4, concat_axis=3, tiled=True
            ),
        )
    )
    mode_count = spec_u.shape[3]
    position = jnp.arange(mode_count, dtype=jnp.int32)
    kxz_index = lax.axis_index("space") * (mode_count // (2 * MY)) + position // (2 * MY)
    mode_weights = jnp.where(kxz_index % MZ == 0, 1.0, 2.0).astype(jnp.float32) / float(
        NX * NY * NZ
    )
    mode_grad = lax.psum_scatter(
        cross_terms(spec_u, spec_e), "batch", scatter_dimension=2, tiled=True
    )
    grad_spectral = mode_grad * mode_weights
    rounded = spec_e.astype(jnp.bfloat16)
    weight_real = spectral_weight[0]
    weight_imag = spectral_weight[1]
    back_real = contract(weight_real, rounded[:, :, 0]) + contract(weight_imag, rounded[:, :, 1])
    back_imag = contract(weight_real, rounded[:, :, 1]) - contract(weight_imag, rounded[:, :, 0])
    back_modes = jnp.stack([back_real, back_imag], axis=2) * mode_weights
    shaped = back_modes.reshape(samples, channels, 2, mode_count // (2 * MY), 2 * MY)
    cos_y, sin_y = phase_table(NY, 2 * MY, True)
    grid_y = jnp.einsum("scpmk,pkqy->scqym", shaped, inverse_block(cos_y, sin_y), precision=HIGHEST)
    spatial = to_grid(lax.all_to_all(grid_y, "space", split_axis=3, concat_axis=4, tiled=True))
    mixed = jnp.einsum("io,soxyz->sixyz", skip_weight, cot_pre, preferred_element_type=jnp.float32)
    grad_inputs = (spatial + mixed).astype(jnp.bfloat16)
    grad_skip = skip_gradient(inputs, cot_pre)
    return (grad_inputs, grad_spectral, grad_skip)


def solution(mesh):
    placed = (
        P("batch", None, None, "space", None),
        P("batch", None, None, "space", None),
        P("batch", None, None, "space", None),
        P(None, None, None, "space"),
        P(),
    )
    return jax.shard_map(
        on_device,
        mesh=mesh,
        in_specs=placed,
        out_specs=(P("batch", None, None, "space", None), P(None, None, "batch", "space"), P()),
        check_vma=False,
    )
```

profile of v0, /device:TPU:2, one launch (start us, length us, event | category | flops | bytes accessed | tf_op | source)
XLA Modules:
  0.0 209.4 jit_solution(695585654018447)
XLA Ops:
  7.5 2.3 %fusion.8 = bf16[1,32,128,1,128]{4,2,3,1,0:T(8,128)(2,1)S(1)} fusion(bf16[1,32,128,1,128]{4,2,3,1,0:T(8,128)(2,1)} %param.6, bf16[1,32,128,1,128]{4,2,3,1,0:T(8,128)(2,1)} %param.7), kind=kLoop, calls=%fused_computation.13 | loop fusion | flops 6291456 | bytes 3145728 | tf_op jit(solution)/shard_map/convert_element_type | solution.py:116
  10.1 2.5 %convolution_bitcast_fusion.4 = f32[1,32,2,1,32,16]{4,5,1,2,3,0:T(8,128)S(1)} fusion(f32[32,2,32,128]{3,2,0,1:T(8,128)S(1)} %convolution_bitcast_fusion.2, f32[1,128,2,16]{1,3,0,2:T(8,128)S(1)} %get-tuple-element.33, f32[1,128,2,16]{1,3,0,2:T(8,128)S(1)} %get-tuple-element.32), kind=kOutput, calls=%fused_computation.19 | convolution fusion | flops 100671488 | bytes 1212416 | tf_op jit(solution)/shard_map/scpayz,pzqk->scqyak/dot_general | solution.py:53
  12.9 0.4 copy.162
  13.3 1.2 reshape.693
  14.5 18.7 %all-to-all-start = ((f32[128,1,256]{2,1,0:T(1,128)}), f32[128,1,256]{2,1,0:T(1,128)S(1)}, u32[]{:S(2)}, u32[]{:S(2)}) async-start(f32[128,1,256]{2,1,0:T(1,128)} %reshape.693), calls=%async_computation | async-start | bytes 262144 | tf_op jit(solution)/shard_map/all_to_all | solution.py:122
  33.9 2.5 %convolution_bitcast_fusion.3 = f32[1,32,2,1,32,16]{4,5,1,2,3,0:T(8,128)S(1)} fusion(f32[32,2,32,128]{3,2,0,1:T(8,128)S(1)} %convolution_bitcast_fusion.1, f32[1,128,2,16]{1,3,0,2:T(8,128)S(1)} %get-tuple-element.33, f32[1,128,2,16]{1,3,0,2:T(8,128)S(1)} %get-tuple-element.32), kind=kOutput, calls=%fused_computation.18 | convolution fusion | flops 100671488 | bytes 1212416 | tf_op jit(solution)/shard_map/scpayz,pzqk->scqyak/dot_general | solution.py:53
  36.4 1.3 convolution_bitcast_fusion.6
  37.7 2.1 fusion.18
  40.5 1.2 reshape.697
  41.7 96.8 %psum.7 = f32[32,32]{0,1:T(8,128)S(1)} all-reduce(f32[32,32]{0,1:T(8,128)S(1)} %convolution_bitcast_fusion.6), channel_id=1, replica_groups=mesh['batch'=4,'space'=128] {'batch','space'}, use_global_device_ids=true, to_apply=%region_1.2 | all-reduce | flops 1024 | bytes 8192 | tf_op jit(solution)/shard_map/psum | solution.py:108
  138.6 11.8 %all-to-all-start.2 = ((f32[128,1,256]{2,1,0:T(1,128)}), f32[128,1,256]{2,1,0:T(1,128)S(1)}, u32[]{:S(2)}, u32[]{:S(2)}) async-start(f32[128,1,256]{2,1,0:T(1,128)} %reshape.697), calls=%async_computation.2 | async-start | bytes 262144 | tf_op jit(solution)/shard_map/all_to_all | solution.py:119
  150.4 0.5 broadcast.824
  150.9 0.9 reduce.8
  151.9 0.4 reshape.694
  152.6 0.5 fusion.28
  153.2 9.8 %all-to-all-done.2 = f32[128,1,256]{2,1,0:T(1,128)S(1)} async-done(((f32[128,1,256]{2,1,0:T(1,128)}), f32[128,1,256]{2,1,0:T(1,128)S(1)}, u32[]{:S(2)}, u32[]{:S(2)}) %all-to-all-start.2) | async-done | bytes 131104 | tf_op jit(solution)/shard_map/all_to_all | solution.py:119
  163.0 0.9 reduce.10
  163.9 0.4 reshape.698
  164.7 0.5 fusion.25
  165.5 1.1 pad_maximum_fusion
  166.8 0.4 fusion.22
  168.1 1.0 reshape.695
  169.1 7.0 %all-to-all-start.1 = ((f32[128,1,256]{2,1,0:T(1,128)}), f32[128,1,256]{2,1,0:T(1,128)S(1)}, u32[]{:S(2)}, u32[]{:S(2)}) async-start(f32[128,1,256]{2,1,0:T(1,128)} %reshape.695), calls=%async_computation.1 | async-start | bytes 262144 | tf_op jit(solution)/shard_map/all_to_all | solution.py:146
  176.2 0.7 copy.80
  177.0 11.7 %all-to-all-done.1 = f32[128,1,256]{2,1,0:T(1,128)S(1)} async-done(((f32[128,1,256]{2,1,0:T(1,128)}), f32[128,1,256]{2,1,0:T(1,128)S(1)}, u32[]{:S(2)}, u32[]{:S(2)}) %all-to-all-start.1) | async-done | bytes 131104 | tf_op jit(solution)/shard_map/all_to_all | solution.py:146
  188.7 0.9 reduce.9
  189.7 1.0 reshape.696
  190.7 1.9 copy.62
  192.6 2.3 %copy.63 = f32[32,2,32,16]{2,3,1,0:T(8,128)} copy(f32[32,2,32,16]{0,3,2,1:T(8,128)} %bitcast.256) | data formatting | bytes 262144 | tf_op jit(solution)/shard_map/reshape.31
  194.9 2.1 convolution_bitcast_fusion
  197.0 3.9 %fusion.9 = bf16[1,32,128,1,128]{4,2,3,1,0:T(8,128)(2,1)} fusion(f32[128,128,32]{1,2,0:T(8,128)S(1)} %copy-done.1, f32[32,2,32,128]{3,2,0,1:T(8,128)S(1)} %convolution_bitcast_fusion, f32[1,32,128]{2,1,0:T(8,128)S(1)} %get-tuple-element.35, f32[1,32,128]{2,1,0:T(8,128)S(1)} %get-tuple-element.34), kind=kOutput, calls=%fused_computation.15 | convolution fusion | flops 403709952 | bytes 4227072 | tf_op jit(solution)/shard_map/scpayz,pax->scxyz/dot_general | solution.py:81
  200.9 1.7 broadcast_multiply_fusion
  (52 shorter events, 4.6 us)
Async XLA Ops:
  7.2 26.4 %copy-start = (bf16[1,32,128,1,128]{4,2,3,1,0:T(8,128)(2,1)S(1)}, bf16[1,32,128,1,128]{4,2,3,1,0:T(8,128)(2,1)}, u32[]{:S(2)}) copy-start(bf16[1,32,128,1,128]{4,2,3,1,0:T(8,128)(2,1)} %param.5) | copy-start | bytes 3145732
  14.5 124.0 %all-to-all-start = ((f32[128,1,256]{2,1,0:T(1,128)}), f32[128,1,256]{2,1,0:T(1,128)S(1)}, u32[]{:S(2)}, u32[]{:S(2)}) async-start(f32[128,1,256]{2,1,0:T(1,128)} %reshape.693), calls=%async_computation | async-start | bytes 262144 | tf_op jit(solution)/shard_map/all_to_all | solution.py:122
  33.9 3.8 %copy-start.3 = (bf16[32,32]{1,0:T(8,128)(2,1)S(1)}, bf16[32,32]{1,0:T(8,128)(2,1)}, u32[]{:S(2)}) copy-start(bf16[32,32]{1,0:T(8,128)(2,1)} %param.9) | copy-start | bytes 6148
  138.6 24.4 %all-to-all-start.2 = ((f32[128,1,256]{2,1,0:T(1,128)}), f32[128,1,256]{2,1,0:T(1,128)S(1)}, u32[]{:S(2)}, u32[]{:S(2)}) async-start(f32[128,1,256]{2,1,0:T(1,128)} %reshape.697), calls=%async_computation.2 | async-start | bytes 262144 | tf_op jit(solution)/shard_map/all_to_all | solution.py:119
  150.4 50.5 %reduce-scatter.2.cloned.1.call-start = ((), (), s32[]{:S(2)}) async-start(), calls=%async_computation.4 | async-start | bytes 1310720 | tf_op jit(solution)/shard_map/reduce_scatter | solution.py:133
  165.5 1.3 copy-start.2
  169.1 19.6 %all-to-all-start.1 = ((f32[128,1,256]{2,1,0:T(1,128)}), f32[128,1,256]{2,1,0:T(1,128)S(1)}, u32[]{:S(2)}, u32[]{:S(2)}) async-start(f32[128,1,256]{2,1,0:T(1,128)} %reshape.695), calls=%async_computation.1 | async-start | bytes 262144 | tf_op jit(solution)/shard_map/all_to_all | solution.py:146
  189.7 7.3 %copy-start.1 = (f32[128,128,32]{1,2,0:T(8,128)S(1)}, f32[128,128,32]{1,2,0:T(8,128)}, u32[]{:S(2)}) copy-start(f32[128,128,32]{1,2,0:T(8,128)} %fusion.18) | copy-start | bytes 6291460
Sparse Core Ops, SparseCore 0:
  166.7 31.4 reduce-scatter.1
where the time goes:
time: 210 us; the launch traced here: 209 us
  blocking collectives  96.8 us (46%)
  starting transfers between devices  37.6 us (18%)
  waiting for transfers between devices  21.5 us (10%)
  matrix products  16.1 us (8%)
  between operations  14.4 us (7%)
  local copies, waits for them, and re-layouts  13.7 us (7%)
  other arithmetic  9.26 us (4%)
    psum x1, blocking collectives, skip_gradient(): summed = lax.psum(partial_sum, ('batch', 'space'))  96.8 us
    all_to_all x1, starting transfers between devices, on_device(): lax.all_to_all(local_spectrum(cot_pre), 'space', split_axis=4, concat_axi...  18.7 us
    all_to_all x1, starting transfers between devices, on_device(): lax.all_to_all(local_spectrum(inputs), 'space', split_axis=4, concat_axis...  11.8 us
    all_to_all x1, waiting for transfers between devices, on_device(): lax.all_to_all(grid_y, 'space', split_axis=3, concat_axis=4, tiled=True)  11.7 us
    all_to_all x1, waiting for transfers between devices, on_device(): lax.all_to_all(local_spectrum(inputs), 'space', split_axis=4, concat_axis...  9.75 us
    all_to_all x1, starting transfers between devices, on_device(): lax.all_to_all(grid_y, 'space', split_axis=3, concat_axis=4, tiled=True)  7.05 us
    unnamed x17, local copies, waits for them, and re-layouts  6.13 us
    dot_general x2, matrix products, local_spectrum(): jnp.einsum('scpayz,pzqk->scqyak', section_x, forward_block(cos_z, sin_z),...  4.95 us
  transfers between devices with their start and end apart: 4, of which 2 were waited for; matrix products, arithmetic and copies ran while one was open for 13% of the time, Pallas kernels for 0%

commit v1 on v0

--- a/solution.py
+++ b/solution.py
@@ -105,7 +105,7 @@
     partial_sum = jnp.einsum(
         "sixyz,soxyz->io", grid_in, cot_pre, preferred_element_type=jnp.float32
     )
-    summed = lax.psum(partial_sum, ("batch", "space"))
+    summed = lax.psum(lax.psum(partial_sum, "batch"), "space")
     return summed / math.sqrt(grid_in.shape[0] * lax.axis_size("batch") * NX * NY * NZ)
 
 

time: 210 us -> 732 us (3.49)
  the two profiles are of different devices: /device:TPU:2 before, /device:TPU:1 now
where the time goes in v1:
time: 732 us; the launch traced here: 731 us
  blocking collectives  513 us (70%)
  waiting for transfers between devices  134 us (18%)
  starting transfers between devices  31.9 us (4%)
  matrix products  16.1 us (2%)
  between operations  14.4 us (2%)
  local copies, waits for them, and re-layouts  13.7 us (2%)
  other arithmetic  9.01 us (1%)
    psum x2, blocking collectives, skip_gradient(): summed = lax.psum(lax.psum(partial_sum, 'batch'), 'space')  513 us
    reduce_scatter x1, waiting for transfers between devices, on_device(): lax.psum_scatter(cross_terms(spec_u, spec_e), 'batch', scatter_dimension=...  113 us
    all_to_all x1, starting transfers between devices, on_device(): lax.all_to_all(local_spectrum(cot_pre), 'space', split_axis=4, concat_axi...  19.3 us
  transfers between devices with their start and end apart: 4, of which 3 were waited for; matrix products, arithmetic and copies ran while one was open for 4% of the time, Pallas kernels for 0%

profile of v1, /device:TPU:1, one launch (start us, length us, event | category | flops | bytes accessed | tf_op | source)
XLA Modules:
  0.0 731.3 jit_solution(12757816285861513812)
XLA Ops:
  7.5 2.3 fusion.8
  10.1 2.5 convolution_bitcast_fusion.4
  13.3 1.2 reshape.693
  14.5 19.3 %all-to-all-start = ((f32[128,1,256]{2,1,0:T(1,128)}), f32[128,1,256]{2,1,0:T(1,128)S(1)}, u32[]{:S(2)}, u32[]{:S(2)}) async-start(f32[128,1,256]{2,1,0:T(1,128)} %reshape.693), calls=%async_computation | async-start | bytes 262144 | tf_op jit(solution)/shard_map/all_to_all | solution.py:122
  34.5 2.5 convolution_bitcast_fusion.3
  36.9 1.3 convolution_bitcast_fusion.6
  38.2 2.1 fusion.18
  41.1 1.2 reshape.697
  42.3 12.6 %psum.14 = f32[32,32]{0,1:T(8,128)S(1)} all-reduce(f32[32,32]{0,1:T(8,128)S(1)} %convolution_bitcast_fusion.6), channel_id=1, replica_groups=mesh['batch'=4,'space'=128] {'batch'}, use_global_device_ids=true, to_apply=%region_1.2 | all-reduce | flops 1024 | bytes 8192 | tf_op jit(solution)/shard_map/psum | solution.py:108
  54.9 500.0 %psum.15 = f32[32,32]{0,1:T(8,128)S(1)} all-reduce(f32[32,32]{0,1:T(8,128)S(1)} %psum.14), channel_id=1, replica_groups=mesh['batch'=4,'space'=128] {'space'}, use_global_device_ids=true, to_apply=%region_2.3 | all-reduce | flops 1024 | bytes 8192 | tf_op jit(solution)/shard_map/psum | solution.py:108
  555.0 6.2 all-to-all-start.2
  561.2 0.5 broadcast.824
  561.7 0.8 reduce.8
  562.5 0.4 reshape.694
  563.3 0.5 fusion.28
  563.9 9.6 %all-to-all-done.2 = f32[128,1,256]{2,1,0:T(1,128)S(1)} async-done(((f32[128,1,256]{2,1,0:T(1,128)}), f32[128,1,256]{2,1,0:T(1,128)S(1)}, u32[]{:S(2)}, u32[]{:S(2)}) %all-to-all-start.2) | async-done | bytes 131104 | tf_op jit(solution)/shard_map/all_to_all | solution.py:119
  573.5 0.8 reduce.10
  574.3 0.4 reshape.698
  575.1 0.5 fusion.25
  575.9 1.1 pad_maximum_fusion
  578.4 1.0 reshape.695
  579.4 6.4 all-to-all-start.1
  585.9 0.7 copy.80
  586.7 11.2 %all-to-all-done.1 = f32[128,1,256]{2,1,0:T(1,128)S(1)} async-done(((f32[128,1,256]{2,1,0:T(1,128)}), f32[128,1,256]{2,1,0:T(1,128)S(1)}, u32[]{:S(2)}, u32[]{:S(2)}) %all-to-all-start.1) | async-done | bytes 131104 | tf_op jit(solution)/shard_map/all_to_all | solution.py:146
  597.9 0.8 reduce.9
  598.8 1.0 reshape.696
  599.8 1.9 copy.62
  601.8 2.3 copy.63
  604.0 2.1 convolution_bitcast_fusion
  606.1 3.9 fusion.9
  610.0 112.8 %reduce-scatter.2.cloned.1.call-done = f32[2,32,8,128]{3,2,1,0:T(8,128)} async-done(((f32[2,32,32,128]{3,2,1,0:T(8,128)}), f32[2,32,8,128]{3,2,1,0:T(8,128)}) %reduce-scatter.2.cloned.1.call-update) | async-done | bytes 262160 | tf_op jit(solution)/shard_map/reduce_scatter | solution.py:133
  722.8 1.7 broadcast_multiply_fusion
  (53 shorter events, 5.4 us)
Async XLA Ops:
  7.2 27.0 %copy-start = (bf16[1,32,128,1,128]{4,2,3,1,0:T(8,128)(2,1)S(1)}, bf16[1,32,128,1,128]{4,2,3,1,0:T(8,128)(2,1)}, u32[]{:S(2)}) copy-start(bf16[1,32,128,1,128]{4,2,3,1,0:T(8,128)(2,1)} %param.5) | copy-start | bytes 3145732
  14.5 540.4 %all-to-all-start = ((f32[128,1,256]{2,1,0:T(1,128)}), f32[128,1,256]{2,1,0:T(1,128)S(1)}, u32[]{:S(2)}, u32[]{:S(2)}) async-start(f32[128,1,256]{2,1,0:T(1,128)} %reshape.693), calls=%async_computation | async-start | bytes 262144 | tf_op jit(solution)/shard_map/all_to_all | solution.py:122
  34.4 3.8 copy-start.3
  555.0 18.5 %all-to-all-start.2 = ((f32[128,1,256]{2,1,0:T(1,128)}), f32[128,1,256]{2,1,0:T(1,128)S(1)}, u32[]{:S(2)}, u32[]{:S(2)}) async-start(f32[128,1,256]{2,1,0:T(1,128)} %reshape.697), calls=%async_computation.2 | async-start | bytes 262144 | tf_op jit(solution)/shard_map/all_to_all | solution.py:119
  561.1 161.7 %reduce-scatter.2.cloned.1.call-start = ((), (), s32[]{:S(2)}) async-start(), calls=%async_computation.4 | async-start | bytes 1310720 | tf_op jit(solution)/shard_map/reduce_scatter | solution.py:133
  575.9 1.3 copy-start.2
  579.4 18.5 %all-to-all-start.1 = ((f32[128,1,256]{2,1,0:T(1,128)}), f32[128,1,256]{2,1,0:T(1,128)S(1)}, u32[]{:S(2)}, u32[]{:S(2)}) async-start(f32[128,1,256]{2,1,0:T(1,128)} %reshape.695), calls=%async_computation.1 | async-start | bytes 262144 | tf_op jit(solution)/shard_map/all_to_all | solution.py:146
  598.8 7.3 %copy-start.1 = (f32[128,128,32]{1,2,0:T(8,128)S(1)}, f32[128,128,32]{1,2,0:T(8,128)}, u32[]{:S(2)}) copy-start(f32[128,128,32]{1,2,0:T(8,128)} %fusion.18) | copy-start | bytes 6291460
Sparse Core Ops, SparseCore 0:
  577.1 145.6 reduce-scatter.1
